TPU v7x, 32 devices: a whole 2x2x4 slice. The times are simulated.
32 devices in a mesh: dap: 8 (over y, x, core), dp: 4 (over z).
Axes of the slice: x: 2, y: 2, z: 4, core: 2. Of those that a mesh axis runs over, the one named last changes fastest.
Arguments:
- pair: bfloat16 [64, 16, 128], P(('dp', 'dap')), parts along dimension 0, may hold values from -6 to 6
- pair_mask: int32 [64, 16], P(('dp', 'dap')), parts along dimension 0, may hold values from 0 to 1, as said below
- w_left: bfloat16 [128, 256], replicated, may hold values from -0.5 to 0.5
- w_right: bfloat16 [128, 256], replicated, may hold values from -0.5 to 0.5
- w_tri_gate: bfloat16 [128, 128], replicated, may hold values from -0.5 to 0.5
- w_tri_out: bfloat16 [128, 128], replicated, may hold values from -0.5 to 0.5
- w_attend: bfloat16 [128, 512], replicated, may hold values from -0.5 to 0.5
- w_bias: bfloat16 [128, 4], replicated
- w_att_out: bfloat16 [128, 128], replicated, may hold values from -0.5 to 0.5
Outputs:
- pair_out: float32 [64, 16, 128], P('dp', 'dap'), parts along dimension 0
There are 4 independent parts, one for each index of `dp`. A program takes and returns all parts, laid end to end along the dimension named above; an argument that names none is the same for every part. Nothing has to cross between parts.
Inputs may be any that keep to these rules, and one draw needn't show every extreme that they name: pair_mask[i, i] = 1 for every residue i.
All inputs are finite; a program needn't handle non-finite values.
Results may differ from a plain program's by a relative error of at most 0.014.
The roundings to bfloat16 on the way count: a program that leaves them out, or rounds other values in their place, can miss the bound.
Values may be sent and summed in bfloat16 or wider, within the bound.
No kernel may reach another device: no remote copies, remote signals or barrier semaphores. Data moves between devices by JAX's collectives and lax.ppermute only.
A program may use at most 128 MiB of HBM per device.

v0:
```python
import jax
import jax.numpy as jnp
from jax import lax
from jax.sharding import PartitionSpec as P


def layer_norm(x):
    x = x.astype(jnp.float32)
    mean = jnp.mean(x, axis=-1, keepdims=True)
    var = jnp.mean((x - mean) * (x - mean), axis=-1, keepdims=True)
    return (x - mean) / jnp.sqrt(var + 1e-05)


def matmul(x, w):
    flat = x.reshape(-1, x.shape[-1])
    return jnp.dot(flat, w, preferred_element_type=jnp.float32).reshape(
        x.shape[:-1] + (w.shape[1],)
    )


def edges(zn, weight, maskf, hidden):
    both = matmul(zn, weight)
    return (jax.nn.sigmoid(both[..., :hidden]) * both[..., hidden:] * maskf[..., None]).astype(
        jnp.bfloat16
    )


def triangle_update(pair_part, zn_part, tri, w_tri_gate, w_tri_out):
    tn = layer_norm(tri).astype(jnp.bfloat16)
    update = jax.nn.sigmoid(matmul(zn_part, w_tri_gate)) * matmul(tn, w_tri_out)
    return pair_part.astype(jnp.float32) + update


def attention(pair1, mask_cols, w_attend, w_bias, w_att_out):
    inner = w_att_out.shape[0]
    heads = w_bias.shape[1]
    head_dim = inner // heads
    total, local = (pair1.shape[0], pair1.shape[1])
    yn = layer_norm(pair1).astype(jnp.bfloat16)
    proj = matmul(yn, w_attend)
    query = proj[..., :inner].astype(jnp.bfloat16).reshape(total, local, heads, head_dim)
    keys = proj[..., inner : 2 * inner].astype(jnp.bfloat16).reshape(total, local, heads, head_dim)
    values = (
        proj[..., 2 * inner : 3 * inner].astype(jnp.bfloat16).reshape(total, local, heads, head_dim)
    )
    gate = jax.nn.sigmoid(proj[..., 3 * inner :])
    bias_part = jnp.einsum("kic,ch->hki", yn, w_bias, preferred_element_type=jnp.float32).astype(
        jnp.bfloat16
    )
    bias = lax.all_gather(bias_part, "dap", axis=2, tiled=True)
    scores = jnp.einsum(
        "irhd,krhd->rhki", query, keys, preferred_element_type=jnp.float32
    ) / jnp.sqrt(jnp.float32(head_dim))
    scores = scores + bias.astype(jnp.float32)[None]
    live = jnp.transpose(mask_cols.astype(jnp.float32))[:, None, :, None]
    scores = jnp.where(live > 0.5, scores, jnp.float32(-1000000000.0))
    weights = jax.nn.softmax(scores, axis=2).astype(jnp.bfloat16)
    summed = jnp.einsum(
        "rhki,krhd->irhd", weights, values, preferred_element_type=jnp.float32
    ).reshape(total, local, inner)
    att = (gate * summed).astype(jnp.bfloat16)
    return pair1 + matmul(att, w_att_out)


def shards(pair, pair_mask, w_left, w_right, w_tri_gate, w_tri_out, w_attend, w_bias, w_att_out):
    hidden = w_tri_out.shape[0]
    maskf = pair_mask.astype(jnp.float32)
    zn = layer_norm(pair).astype(jnp.bfloat16)
    left_edge = edges(zn, w_left, maskf, hidden)
    right_edge = edges(zn, w_right, maskf, hidden)
    pair_cols, mask_cols = (
        lax.all_to_all(pair, "dap", split_axis=1, concat_axis=0, tiled=True),
        lax.all_to_all(
            pair_mask.astype(jnp.bfloat16), "dap", split_axis=1, concat_axis=0, tiled=True
        ),
    )
    tri = jnp.einsum(
        "ikc,jkc->ijc",
        lax.all_gather(left_edge, "dap", axis=0, tiled=True),
        right_edge,
        preferred_element_type=jnp.float32,
    )
    zn_cols = layer_norm(pair_cols).astype(jnp.bfloat16)
    pair1 = triangle_update(pair_cols, zn_cols, tri, w_tri_gate, w_tri_out)
    return attention(pair1, mask_cols, w_attend, w_bias, w_att_out)


def solution(mesh):
    placed = (
        P(("dp", "dap"), None, None),
        P(("dp", "dap"), None),
        P(),
        P(),
        P(),
        P(),
        P(),
        P(),
        P(),
    )
    return jax.shard_map(
        shards, mesh=mesh, in_specs=placed, out_specs=P("dp", "dap", None), check_vma=False
    )
```

profile of v0, /device:TPU:0, one launch (start us, length us, event | category | flops | bytes accessed | tf_op | source)
XLA Modules:
  0.0 41.4 jit_solution(9851496634011292177)
XLA Ops:
  0.0 0.8 %fusion.56 = (bf16[2,16]{1,0:T(2,128)(2,1)S(1)}, f32[2,16]{1,0:T(2,128)S(1)}) fusion(s32[2,16]{1,0:T(2,128)} %param.10), kind=kLoop, calls=%fused_computation.85 | loop fusion | flops 64 | bytes 320 | tf_op jit(solution)/shard_map/convert_element_type | solution.py:74
  0.8 0.6 %copy.53 = bf16[2,8,2]{2,0,1:T(2,128)(2,1)} copy(bf16[2,8,2]{2,1,0:T(8,128)(2,1)S(1)} %all_to_all.8) | data formatting | bytes 128 | tf_op jit(solution)/shard_map/all_to_all | solution.py:73
  1.5 5.2 %all-to-all-start.1 = ((bf16[2,8,2]{2,0,1:T(2,128)(2,1)}), bf16[2,8,2]{2,0,1:T(2,128)(2,1)S(1)}, u32[]{:S(2)}, u32[]{:S(2)}) async-start(bf16[2,8,2]{2,0,1:T(2,128)(2,1)} %copy.53), calls=%async_computation.1 | async-start | bytes 8192 | tf_op jit(solution)/shard_map/all_to_all | solution.py:73
  6.7 0.2 fusion.25
  6.9 1.1 %fusion.12 = f32[2,16,256]{2,1,0:T(8,128)S(1)} fusion(bf16[128,256]{1,0:T(8,128)(2,1)} %param.11, bf16[2,16,128]{2,1,0:T(8,128)(2,1)S(1)} %copy-done.1, f32[2,16]{1,0:T(2,128)S(1)} %add_sqrt_fusion.3, f32[2,16]{1,0:T(2,128)S(1)} %broadcast_multiply_fusion.3), kind=kOutput, calls=%fused_computation.18 | convolution fusion | flops 2113536 | bytes 106752 | tf_op jit(solution)/shard_map/dot_general | solution.py:16
  8.0 0.2 fusion.14
  8.3 9.7 %all_gather.6 = bf16[16,16,128]{2,1,0:T(8,128)(2,1)S(1)} all-gather(bf16[2,16,128]{2,1,0:T(8,128)(2,1)S(1)} %get-tuple-element.10), channel_id=1, replica_groups=mesh['dap'=8,'dp'=4] {'dap'}, dimensions={0}, use_global_device_ids=true | all-gather | bytes 73728 | tf_op jit(solution)/shard_map/all_gather | solution.py:79
  18.0 0.4 %copy.51 = bf16[16,16,128]{1,0,2:T(8,128)(2,1)S(1)} copy(bf16[16,16,128]{2,1,0:T(8,128)(2,1)S(1)} %all_gather.6) | data formatting | bytes 131072 | tf_op jit(solution)/shard_map/all_gather | solution.py:79
  18.4 0.1 copy.50
  18.6 0.4 fusion.60
  19.1 0.2 multiply_reduce_fusion.1
  19.3 0.6 %copy.48 = bf16[2,16,128]{2,0,1:T(2,128)(2,1)} copy(bf16[2,16,128]{2,1,0:T(8,128)(2,1)S(1)} %copy-done.1) | data formatting | bytes 16384 | tf_op args[0]
  19.9 3.3 %all-to-all-start = ((bf16[2,16,128]{2,0,1:T(2,128)(2,1)}), bf16[2,16,128]{2,0,1:T(2,128)(2,1)S(1)}, u32[]{:S(2)}, u32[]{:S(2)}) async-start(bf16[2,16,128]{2,0,1:T(2,128)(2,1)} %copy.48), calls=%async_computation | async-start | bytes 16384 | tf_op jit(solution)/shard_map/all_to_all | solution.py:72
  23.3 0.1 copy.63
  23.4 4.5 %all-to-all-done = bf16[2,16,128]{2,0,1:T(2,128)(2,1)S(1)} async-done(((bf16[2,16,128]{2,0,1:T(2,128)(2,1)}), bf16[2,16,128]{2,0,1:T(2,128)(2,1)S(1)}, u32[]{:S(2)}, u32[]{:S(2)}) %all-to-all-start) | async-done | bytes 8224 | tf_op jit(solution)/shard_map/all_to_all | solution.py:72
  28.0 0.2 fusion.42
  28.4 0.6 %copy-done.5 = bf16[128,128]{1,0:T(8,128)(2,1)S(1)} copy-done((bf16[128,128]{1,0:T(8,128)(2,1)S(1)}, bf16[128,128]{1,0:T(8,128)(2,1)}, u32[]{:S(2)}) %copy-start.5) | copy-done | bytes 32792
  29.0 0.2 fusion.8
  29.2 0.6 %copy-done.6 = bf16[128,128]{1,0:T(8,128)(2,1)S(1)} copy-done((bf16[128,128]{1,0:T(8,128)(2,1)S(1)}, bf16[128,128]{1,0:T(8,128)(2,1)}, u32[]{:S(2)}) %copy-start.6) | copy-done | bytes 32792
  29.7 0.3 fusion.57
  30.0 0.2 multiply_reduce_fusion
  30.3 0.1 fusion.58
  30.6 0.6 %copy-done.3 = bf16[128,4]{0,1:T(4,128)(2,1)S(1)} copy-done((bf16[128,4]{0,1:T(4,128)(2,1)S(1)}, bf16[128,4]{0,1:T(4,128)(2,1)}, u32[]{:S(2)}) %copy-start.3) | copy-done | bytes 1048
  31.2 0.1 fusion.9
  31.3 8.0 %all_gather.7 = bf16[4,16,16]{1,0,2:T(4,128)(2,1)S(1)} all-gather(bf16[4,16,2]{1,0,2:T(4,128)(2,1)S(1)} %fusion.9), channel_id=1, replica_groups=mesh['dap'=8,'dp'=4] {'dap'}, dimensions={2}, use_global_device_ids=true | all-gather | bytes 2304 | tf_op jit(solution)/shard_map/all_gather | solution.py:50
  39.3 0.1 copy.57
  39.4 0.1 fusion.4
  39.7 0.2 convolution_bitcast_fusion
  39.9 0.1 reshape.137
  40.0 0.7 %copy-done.2 = bf16[128,128]{1,0:T(8,128)(2,1)S(1)} copy-done((bf16[128,128]{1,0:T(8,128)(2,1)S(1)}, bf16[128,128]{1,0:T(8,128)(2,1)}, u32[]{:S(2)}) %copy-start.2) | copy-done | bytes 32792
  40.7 0.1 convolution_add_fusion
  40.8 0.6 %copy.61 = f32[16,2,128]{2,1,0:T(2,128)} copy(f32[16,2,128]{2,0,1:T(8,128)S(1)} %convolution_add_fusion) | data formatting | bytes 32768 | tf_op jit(solution)/shard_map/add | solution.py:62
  (39 shorter events, 1.2 us)
Async XLA Ops:
  0.0 30.3 %copy-start = (bf16[128,512]{1,0:T(8,128)(2,1)S(1)}, bf16[128,512]{1,0:T(8,128)(2,1)}, u32[]{:S(2)}) copy-start(bf16[128,512]{1,0:T(8,128)(2,1)} %param.15) | copy-start | bytes 393220
  0.8 5.8 %copy-start.1 = (bf16[2,16,128]{2,1,0:T(8,128)(2,1)S(1)}, bf16[2,16,128]{2,1,0:T(8,128)(2,1)}, u32[]{:S(2)}) copy-start(bf16[2,16,128]{2,1,0:T(8,128)(2,1)} %param.9) | copy-start | bytes 24580
  1.5 18.5 %all-to-all-start.1 = ((bf16[2,8,2]{2,0,1:T(2,128)(2,1)}), bf16[2,8,2]{2,0,1:T(2,128)(2,1)S(1)}, u32[]{:S(2)}, u32[]{:S(2)}) async-start(bf16[2,8,2]{2,0,1:T(2,128)(2,1)} %copy.53), calls=%async_computation.1 | async-start | bytes 8192 | tf_op jit(solution)/shard_map/all_to_all | solution.py:73
  6.9 1.1 %copy-start.4 = (bf16[128,256]{1,0:T(8,128)(2,1)S(1)}, bf16[128,256]{1,0:T(8,128)(2,1)}, u32[]{:S(2)}) copy-start(bf16[128,256]{1,0:T(8,128)(2,1)} %param.12) | copy-start | bytes 196612
  19.9 8.0 %all-to-all-start = ((bf16[2,16,128]{2,0,1:T(2,128)(2,1)}), bf16[2,16,128]{2,0,1:T(2,128)(2,1)S(1)}, u32[]{:S(2)}, u32[]{:S(2)}) async-start(bf16[2,16,128]{2,0,1:T(2,128)(2,1)} %copy.48), calls=%async_computation | async-start | bytes 16384 | tf_op jit(solution)/shard_map/all_to_all | solution.py:72
  28.2 0.8 %copy-start.5 = (bf16[128,128]{1,0:T(8,128)(2,1)S(1)}, bf16[128,128]{1,0:T(8,128)(2,1)}, u32[]{:S(2)}) copy-start(bf16[128,128]{1,0:T(8,128)(2,1)} %param.13) | copy-start | bytes 98308
  29.0 0.8 %copy-start.6 = (bf16[128,128]{1,0:T(8,128)(2,1)S(1)}, bf16[128,128]{1,0:T(8,128)(2,1)}, u32[]{:S(2)}) copy-start(bf16[128,128]{1,0:T(8,128)(2,1)} %param.14) | copy-start | bytes 98308
  30.5 0.7 %copy-start.3 = (bf16[128,4]{0,1:T(4,128)(2,1)S(1)}, bf16[128,4]{0,1:T(4,128)(2,1)}, u32[]{:S(2)}) copy-start(bf16[128,4]{0,1:T(4,128)(2,1)} %param.16) | copy-start | bytes 3076
  39.9 0.8 %copy-start.2 = (bf16[128,128]{1,0:T(8,128)(2,1)S(1)}, bf16[128,128]{1,0:T(8,128)(2,1)}, u32[]{:S(2)}) copy-start(bf16[128,128]{1,0:T(8,128)(2,1)} %param.17) | copy-start | bytes 98308
where the time goes:
time: 42 us; the launch traced here: 41.4 us
  blocking collectives  17.7 us (42%)
  starting transfers between devices  8.53 us (20%)
  local copies, waits for them, and re-layouts  5.7 us (14%)
  waiting for transfers between devices  4.51 us (11%)
  matrix products  2.83 us (7%)
  other arithmetic  1.97 us (5%)
    all_gather x1, blocking collectives, shards(): lax.all_gather(left_edge, 'dap', axis=0, tiled=True)  9.75 us
    all_gather x1, blocking collectives, attention(): bias = lax.all_gather(bias_part, 'dap', axis=2, tiled=True)  7.98 us
    all_to_all x1, starting transfers between devices, shards(): lax.all_to_all(pair_mask.astype(jnp.bfloat16), 'dap', split_axis=1, conca...  5.2 us
    all_to_all x1, waiting for transfers between devices, shards(): lax.all_to_all(pair, 'dap', split_axis=1, concat_axis=0, tiled=True)  4.51 us
    all_to_all x1, starting transfers between devices, shards(): lax.all_to_all(pair, 'dap', split_axis=1, concat_axis=0, tiled=True)  3.33 us
    unnamed x15, local copies, waits for them, and re-layouts  3 us
    dot_general x6, matrix products, matmul(): jnp.dot(flat, w, preferred_element_type=jnp.float32)  1.99 us
  transfers between devices with their start and end apart: 2, of which 1 were waited for; matrix products, arithmetic and copies ran while one was open for 9% of the time, Pallas kernels for 0%

commit v1 on v0

--- a/solution.py
+++ b/solution.py
@@ -2,6 +2,12 @@
 import jax.numpy as jnp
 from jax import lax
 from jax.sharding import PartitionSpec as P
+
+
+def joined_along(parts, dim):
+    parts = jnp.moveaxis(parts, 0, dim)
+    shape = parts.shape
+    return parts.reshape(*shape[:dim], shape[dim] * shape[dim + 1], *shape[dim + 2 :])
 
 
 def layer_norm(x):
@@ -74,12 +80,18 @@
             pair_mask.astype(jnp.bfloat16), "dap", split_axis=1, concat_axis=0, tiled=True
         ),
     )
-    tri = jnp.einsum(
-        "ikc,jkc->ijc",
-        lax.all_gather(left_edge, "dap", axis=0, tiled=True),
-        right_edge,
-        preferred_element_type=jnp.float32,
-    )
+    size, index, rows = (lax.axis_size("dap"), lax.axis_index("dap"), left_edge.shape[0])
+    right = [(i, (i + 1) % size) for i in range(size)]
+    blocks = []
+    block = left_edge
+    for turn in range(size):
+        upcoming = block if turn == size - 1 else lax.ppermute(block, "dap", right)
+        blocks.append(
+            jnp.einsum("ikc,jkc->ijc", block, right_edge, preferred_element_type=jnp.float32)
+        )
+        block = upcoming
+    blocks = jnp.stack(blocks)[(index - jnp.arange(size)) % size]
+    tri = joined_along(blocks, 0)
     zn_cols = layer_norm(pair_cols).astype(jnp.bfloat16)
     pair1 = triangle_update(pair_cols, zn_cols, tri, w_tri_gate, w_tri_out)
     return attention(pair1, mask_cols, w_attend, w_bias, w_att_out)

time: 42 us -> 62.9 us (1.50)
  waiting for transfers between devices: 4.51 us -> 29.7 us
  blocking collectives: 17.7 us -> 7.97 us
  local copies, waits for them, and re-layouts: 5.7 us -> 8.08 us
  matrix products: 2.83 us -> 5.09 us
  starting transfers between devices: 8.53 us -> 9.17 us
    ppermute x0 -> x7, waiting for transfers between devices: none -> 21.7 us  [shards(): upcoming = block if turn == size - 1 else lax.ppermute(block, 'dap', right)]
    all_gather x1 -> x0, blocking collectives: 9.75 us -> none  [shards(): lax.all_gather(left_edge, 'dap', axis=0, tiled=True)]
    all_to_all x1, waiting for transfers between devices: 0.01 us -> 3.5 us  [shards(): lax.all_to_all(pair_mask.astype(jnp.bfloat16), 'dap', split_axis=1, conca...]
    dot_general x1 -> x8, matrix products: 0.37 us -> 2.63 us  [shards(): jnp.einsum('ikc,jkc->ijc', block, right_edge, preferred_element_type=jnp....]
    ppermute x0 -> x7, local copies, waits for them, and re-layouts: none -> 0.88 us  [shards(): upcoming = block if turn == size - 1 else lax.ppermute(block, 'dap', right)]
    ppermute x0 -> x7, starting transfers between devices: none -> 0.85 us  [shards(): upcoming = block if turn == size - 1 else lax.ppermute(block, 'dap', right)]
    reduce_sum x3, other arithmetic: 0.26 us -> 1.03 us  [layer_norm(): mean = jnp.mean(x, axis=-1, keepdims=True)]
    convert_element_type x1, other arithmetic: 0.76 us -> 0.01 us  [shards(): pair_mask.astype(jnp.bfloat16)]
  transfers between devices with their start and end apart: 2 -> 9, of which waited for: 1 -> 8; matrix products, arithmetic and copies ran while one was open for 9% -> 7% of each run, Pallas kernels for 0% -> 0%
where the time goes in v1:
time: 62.9 us; the launch traced here: 62.4 us
  waiting for transfers between devices  29.7 us (47%)
  starting transfers between devices  9.17 us (15%)
  local copies, waits for them, and re-layouts  8.08 us (13%)
  blocking collectives  7.97 us (13%)
  matrix products  5.09 us (8%)
  other arithmetic  2 us (3%)
    ppermute x7, waiting for transfers between devices, shards(): upcoming = block if turn == size - 1 else lax.ppermute(block, 'dap', right)  21.7 us
    all_gather x1, blocking collectives, attention(): bias = lax.all_gather(bias_part, 'dap', axis=2, tiled=True)  7.97 us
    all_to_all x1, starting transfers between devices, shards(): lax.all_to_all(pair_mask.astype(jnp.bfloat16), 'dap', split_axis=1, conca...  4.99 us
    all_to_all x1, waiting for transfers between devices, shards(): lax.all_to_all(pair, 'dap', split_axis=1, concat_axis=0, tiled=True)  4.51 us
    all_to_all x1, waiting for transfers between devices, shards(): lax.all_to_all(pair_mask.astype(jnp.bfloat16), 'dap', split_axis=1, conca...  3.5 us
    unnamed x17, local copies, waits for them, and re-layouts  3.34 us
    all_to_all x1, starting transfers between devices, shards(): lax.all_to_all(pair, 'dap', split_axis=1, concat_axis=0, tiled=True)  3.33 us
    dot_general x8, matrix products, shards(): jnp.einsum('ikc,jkc->ijc', block, right_edge, preferred_element_type=jnp....  2.63 us
  transfers between devices with their start and end apart: 9, of which 8 were waited for; matrix products, arithmetic and copies ran while one was open for 7% of the time, Pallas kernels for 0%

profile of v1, /device:TPU:0, one launch (start us, length us, event | category | flops | bytes accessed | tf_op | source)
XLA Modules:
  0.0 62.4 jit_solution(12825366767834870501)
XLA Ops:
  0.0 0.9 %convert_reduce_fusion = f32[2,16]{1,0:T(2,128)S(1)} fusion(bf16[2,16,128]{2,1,0:T(8,128)(2,1)} %param.9), kind=kLoop, calls=%fused_computation.48 | loop fusion | flops 8160 | bytes 8320 | tf_op jit(solution)/shard_map/reduce_sum | solution.py:15
  1.0 1.1 %fusion.20 = f32[2,16,256]{2,1,0:T(8,128)S(1)} fusion(bf16[128,256]{1,0:T(8,128)(2,1)} %param.11, bf16[2,16,128]{2,1,0:T(8,128)(2,1)S(1)} %copy-done.1, f32[2,16]{1,0:T(2,128)S(1)} %add_sqrt_fusion.3, f32[2,16]{1,0:T(2,128)S(1)} %broadcast_multiply_fusion.3), kind=kOutput, calls=%fused_computation.35 | convolution fusion | flops 2113536 | bytes 106752 | tf_op jit(solution)/shard_map/dot_general | solution.py:22
  2.3 0.5 copy-done.3
  2.9 0.5 collective-permute-start
  3.5 0.6 copy.254
  4.1 5.0 %all-to-all-start.1 = ((bf16[2,8,2]{2,0,1:T(2,128)(2,1)}), bf16[2,8,2]{2,0,1:T(2,128)(2,1)S(1)}, u32[]{:S(2)}, u32[]{:S(2)}) async-start(bf16[2,8,2]{2,0,1:T(2,128)(2,1)} %copy.254), calls=%async_computation.1 | async-start | bytes 8192 | tf_op jit(solution)/shard_map/all_to_all | solution.py:79
  9.6 0.6 copy.228
  10.2 3.5 %all-to-all-done.1 = bf16[2,8,2]{2,0,1:T(2,128)(2,1)S(1)} async-done(((bf16[2,8,2]{2,0,1:T(2,128)(2,1)}), bf16[2,8,2]{2,0,1:T(2,128)(2,1)S(1)}, u32[]{:S(2)}, u32[]{:S(2)}) %all-to-all-start.1) | async-done | bytes 96 | tf_op jit(solution)/shard_map/all_to_all | solution.py:79
  13.7 3.3 %all-to-all-start = ((bf16[2,16,128]{2,0,1:T(2,128)(2,1)}), bf16[2,16,128]{2,0,1:T(2,128)(2,1)S(1)}, u32[]{:S(2)}, u32[]{:S(2)}) async-start(bf16[2,16,128]{2,0,1:T(2,128)(2,1)} %copy.228), calls=%async_computation | async-start | bytes 16384 | tf_op jit(solution)/shard_map/all_to_all | solution.py:78
  17.2 4.5 %all-to-all-done = bf16[2,16,128]{2,0,1:T(2,128)(2,1)S(1)} async-done(((bf16[2,16,128]{2,0,1:T(2,128)(2,1)}), bf16[2,16,128]{2,0,1:T(2,128)(2,1)S(1)}, u32[]{:S(2)}, u32[]{:S(2)}) %all-to-all-start) | async-done | bytes 8224 | tf_op jit(solution)/shard_map/all_to_all | solution.py:78
  22.2 0.6 copy-done.6
  23.2 0.3 fusion.7
  23.5 3.6 %collective-permute-done.1 = bf16[2,16,128]{2,1,0:T(8,128)(2,1)S(1)} collective-permute-done((bf16[2,16,128]{2,1,0:T(8,128)(2,1)S(1)}, bf16[2,16,128]{2,1,0:T(8,128)(2,1)S(1)}, u32[]{:S(2)}, u32[]{:S(2)}) %collective-permute-start.1) | collective-permute-done | bytes 8224 | tf_op jit(solution)/shard_map/ppermute | solution.py:88
  27.3 0.3 fusion.6
  27.7 3.6 %collective-permute-done.2 = bf16[2,16,128]{2,1,0:T(8,128)(2,1)S(1)} collective-permute-done((bf16[2,16,128]{2,1,0:T(8,128)(2,1)S(1)}, bf16[2,16,128]{2,1,0:T(8,128)(2,1)S(1)}, u32[]{:S(2)}, u32[]{:S(2)}) %collective-permute-start.2) | collective-permute-done | bytes 8224 | tf_op jit(solution)/shard_map/ppermute | solution.py:88
  31.5 0.3 fusion.5
  31.8 3.6 %collective-permute-done.3 = bf16[2,16,128]{2,1,0:T(8,128)(2,1)S(1)} collective-permute-done((bf16[2,16,128]{2,1,0:T(8,128)(2,1)S(1)}, bf16[2,16,128]{2,1,0:T(8,128)(2,1)S(1)}, u32[]{:S(2)}, u32[]{:S(2)}) %collective-permute-start.3) | collective-permute-done | bytes 8224 | tf_op jit(solution)/shard_map/ppermute | solution.py:88
  35.6 0.3 fusion.4
  36.0 3.6 %collective-permute-done.4 = bf16[2,16,128]{2,1,0:T(8,128)(2,1)S(1)} collective-permute-done((bf16[2,16,128]{2,1,0:T(8,128)(2,1)S(1)}, bf16[2,16,128]{2,1,0:T(8,128)(2,1)S(1)}, u32[]{:S(2)}, u32[]{:S(2)}) %collective-permute-start.4) | collective-permute-done | bytes 8224 | tf_op jit(solution)/shard_map/ppermute | solution.py:88
  39.8 0.3 fusion.3
  40.1 3.6 %collective-permute-done.5 = bf16[2,16,128]{2,1,0:T(8,128)(2,1)S(1)} collective-permute-done((bf16[2,16,128]{2,1,0:T(8,128)(2,1)S(1)}, bf16[2,16,128]{2,1,0:T(8,128)(2,1)S(1)}, u32[]{:S(2)}, u32[]{:S(2)}) %collective-permute-start.5) | collective-permute-done | bytes 8224 | tf_op jit(solution)/shard_map/ppermute | solution.py:88
  43.9 0.3 fusion.2
  44.3 3.6 %collective-permute-done.6 = bf16[2,16,128]{2,1,0:T(8,128)(2,1)S(1)} collective-permute-done((bf16[2,16,128]{2,1,0:T(8,128)(2,1)S(1)}, bf16[2,16,128]{2,1,0:T(8,128)(2,1)S(1)}, u32[]{:S(2)}, u32[]{:S(2)}) %collective-permute-start.6) | collective-permute-done | bytes 8224 | tf_op jit(solution)/shard_map/ppermute | solution.py:88
  48.0 0.3 fusion.1
  48.4 0.5 copy.246
  48.8 0.6 gather_fusion
  50.2 0.4 copy-done.7
  50.6 0.3 fusion.69
  51.5 0.6 copy-done.4
  52.2 8.0 %all_gather.3 = bf16[4,16,16]{1,0,2:T(4,128)(2,1)S(1)} all-gather(bf16[4,16,2]{1,0,2:T(4,128)(2,1)S(1)} %fusion.17), channel_id=1, replica_groups=mesh['dap'=8,'dp'=4] {'dap'}, dimensions={2}, use_global_device_ids=true | all-gather | bytes 2304 | tf_op jit(solution)/shard_map/all_gather | solution.py:56
  60.9 0.7 %copy-done.2 = bf16[128,128]{1,0:T(8,128)(2,1)S(1)} copy-done((bf16[128,128]{1,0:T(8,128)(2,1)S(1)}, bf16[128,128]{1,0:T(8,128)(2,1)}, u32[]{:S(2)}) %copy-start.2) | copy-done | bytes 32792
  61.7 0.6 copy.262
  (77 shorter events, 5.4 us)
Async XLA Ops:
  0.0 51.2 %copy-start = (bf16[128,512]{1,0:T(8,128)(2,1)S(1)}, bf16[128,512]{1,0:T(8,128)(2,1)}, u32[]{:S(2)}) copy-start(bf16[128,512]{1,0:T(8,128)(2,1)} %param.15) | copy-start | bytes 393220
  0.0 0.9 %copy-start.1 = (bf16[2,16,128]{2,1,0:T(8,128)(2,1)S(1)}, bf16[2,16,128]{2,1,0:T(8,128)(2,1)}, u32[]{:S(2)}) copy-start(bf16[2,16,128]{2,1,0:T(8,128)(2,1)} %param.9) | copy-start | bytes 24580
  1.0 1.1 %copy-start.5 = (bf16[128,256]{1,0:T(8,128)(2,1)S(1)}, bf16[128,256]{1,0:T(8,128)(2,1)}, u32[]{:S(2)}) copy-start(bf16[128,256]{1,0:T(8,128)(2,1)} %param.12) | copy-start | bytes 196612
  2.1 0.7 %copy-start.3 = (s32[2,16]{1,0:T(2,128)S(1)}, s32[2,16]{1,0:T(2,128)}, u32[]{:S(2)}) copy-start(s32[2,16]{1,0:T(2,128)} %param.10) | copy-start | bytes 388
  2.9 20.1 %collective-permute-start = (bf16[2,16,128]{2,1,0:T(8,128)(2,1)S(1)}, bf16[2,16,128]{2,1,0:T(8,128)(2,1)S(1)}, u32[]{:S(2)}, u32[]{:S(2)}) collective-permute-start(bf16[2,16,128]{2,1,0:T(8,128)(2,1)S(1)} %get-tuple-element.10), channel_id=1, source_target_pairs={{0,4},{4,8},{8,12},{12,16},{16,20},{20,24},{24,28},{28,0},{1,5},{5... | collective-permute-start | bytes 24584 | tf_op jit(solution)/shard_map/ppermute | solution.py:88
  4.1 9.7 %all-to-all-start.1 = ((bf16[2,8,2]{2,0,1:T(2,128)(2,1)}), bf16[2,8,2]{2,0,1:T(2,128)(2,1)S(1)}, u32[]{:S(2)}, u32[]{:S(2)}) async-start(bf16[2,8,2]{2,0,1:T(2,128)(2,1)} %copy.254), calls=%async_computation.1 | async-start | bytes 8192 | tf_op jit(solution)/shard_map/all_to_all | solution.py:79
  13.7 8.0 %all-to-all-start = ((bf16[2,16,128]{2,0,1:T(2,128)(2,1)}), bf16[2,16,128]{2,0,1:T(2,128)(2,1)S(1)}, u32[]{:S(2)}, u32[]{:S(2)}) async-start(bf16[2,16,128]{2,0,1:T(2,128)(2,1)} %copy.228), calls=%async_computation | async-start | bytes 16384 | tf_op jit(solution)/shard_map/all_to_all | solution.py:78
  22.0 0.8 %copy-start.6 = (bf16[128,128]{1,0:T(8,128)(2,1)S(1)}, bf16[128,128]{1,0:T(8,128)(2,1)}, u32[]{:S(2)}) copy-start(bf16[128,128]{1,0:T(8,128)(2,1)} %param.13) | copy-start | bytes 98308
  23.1 4.0 %collective-permute-start.1 = (bf16[2,16,128]{2,1,0:T(8,128)(2,1)S(1)}, bf16[2,16,128]{2,1,0:T(8,128)(2,1)S(1)}, u32[]{:S(2)}, u32[]{:S(2)}) collective-permute-start(bf16[2,16,128]{2,1,0:T(8,128)(2,1)S(1)} %collective-permute-done), channel_id=1, source_target_pairs={{0,4},{4,8},{8,12},{12,16},{16,20},{20,24},{24,28},{28,0},{1,5},{5... | collective-permute-start | bytes 24584 | tf_op jit(solution)/shard_map/ppermute | solution.py:88
  27.3 4.0 %collective-permute-start.2 = (bf16[2,16,128]{2,1,0:T(8,128)(2,1)S(1)}, bf16[2,16,128]{2,1,0:T(8,128)(2,1)S(1)}, u32[]{:S(2)}, u32[]{:S(2)}) collective-permute-start(bf16[2,16,128]{2,1,0:T(8,128)(2,1)S(1)} %collective-permute-done.1), channel_id=1, source_target_pairs={{0,4},{4,8},{8,12},{12,16},{16,20},{20,24},{24,28},{28,0},{1,5},{5... | collective-permute-start | bytes 24584 | tf_op jit(solution)/shard_map/ppermute | solution.py:88
  31.4 4.0 %collective-permute-start.3 = (bf16[2,16,128]{2,1,0:T(8,128)(2,1)S(1)}, bf16[2,16,128]{2,1,0:T(8,128)(2,1)S(1)}, u32[]{:S(2)}, u32[]{:S(2)}) collective-permute-start(bf16[2,16,128]{2,1,0:T(8,128)(2,1)S(1)} %collective-permute-done.2), channel_id=1, source_target_pairs={{0,4},{4,8},{8,12},{12,16},{16,20},{20,24},{24,28},{28,0},{1,5},{5... | collective-permute-start | bytes 24584 | tf_op jit(solution)/shard_map/ppermute | solution.py:88
  35.6 4.0 %collective-permute-start.4 = (bf16[2,16,128]{2,1,0:T(8,128)(2,1)S(1)}, bf16[2,16,128]{2,1,0:T(8,128)(2,1)S(1)}, u32[]{:S(2)}, u32[]{:S(2)}) collective-permute-start(bf16[2,16,128]{2,1,0:T(8,128)(2,1)S(1)} %collective-permute-done.3), channel_id=1, source_target_pairs={{0,4},{4,8},{8,12},{12,16},{16,20},{20,24},{24,28},{28,0},{1,5},{5... | collective-permute-start | bytes 24584 | tf_op jit(solution)/shard_map/ppermute | solution.py:88
  39.7 4.0 %collective-permute-start.5 = (bf16[2,16,128]{2,1,0:T(8,128)(2,1)S(1)}, bf16[2,16,128]{2,1,0:T(8,128)(2,1)S(1)}, u32[]{:S(2)}, u32[]{:S(2)}) collective-permute-start(bf16[2,16,128]{2,1,0:T(8,128)(2,1)S(1)} %collective-permute-done.4), channel_id=1, source_target_pairs={{0,4},{4,8},{8,12},{12,16},{16,20},{20,24},{24,28},{28,0},{1,5},{5... | collective-permute-start | bytes 24584 | tf_op jit(solution)/shard_map/ppermute | solution.py:88
  43.9 4.0 %collective-permute-start.6 = (bf16[2,16,128]{2,1,0:T(8,128)(2,1)S(1)}, bf16[2,16,128]{2,1,0:T(8,128)(2,1)S(1)}, u32[]{:S(2)}, u32[]{:S(2)}) collective-permute-start(bf16[2,16,128]{2,1,0:T(8,128)(2,1)S(1)} %collective-permute-done.5), channel_id=1, source_target_pairs={{0,4},{4,8},{8,12},{12,16},{16,20},{20,24},{24,28},{28,0},{1,5},{5... | collective-permute-start | bytes 24584 | tf_op jit(solution)/shard_map/ppermute | solution.py:88
  49.9 0.8 %copy-start.7 = (bf16[128,128]{1,0:T(8,128)(2,1)S(1)}, bf16[128,128]{1,0:T(8,128)(2,1)}, u32[]{:S(2)}) copy-start(bf16[128,128]{1,0:T(8,128)(2,1)} %param.14) | copy-start | bytes 98308
  51.4 0.7 %copy-start.4 = (bf16[128,4]{0,1:T(4,128)(2,1)S(1)}, bf16[128,4]{0,1:T(4,128)(2,1)}, u32[]{:S(2)}) copy-start(bf16[128,4]{0,1:T(4,128)(2,1)} %param.16) | copy-start | bytes 3076
  60.8 0.8 %copy-start.2 = (bf16[128,128]{1,0:T(8,128)(2,1)S(1)}, bf16[128,128]{1,0:T(8,128)(2,1)}, u32[]{:S(2)}) copy-start(bf16[128,128]{1,0:T(8,128)(2,1)} %param.17) | copy-start | bytes 98308
